TPU v7x, 256 devices: a whole 4x4x8 slice. The times are simulated.
256 devices in a mesh: px: 16 (over z, core), py: 16 (over x, y).
Axes of the slice: x: 4, y: 4, z: 8, core: 2. Of those that a mesh axis runs over, the one named last changes fastest.
Arguments:
- right_side: float32 [64, 128, 1024], P('px', 'py'), may hold values from -40 to 40
- diagonal: float32 [64, 128, 1024], P('px', 'py'), may hold values from 0.05 to 3
- aggregate_id: int32 [64, 128, 1024], P('px', 'py'), may hold values from 0 to 511, as said below
- coarse_diag: float32 [32, 32, 128], P('px', 'py'), may hold values from 150 to 230
- coarse_link: float32 [3, 32, 32, 128], P(None, 'px', 'py'), may hold values from 0.75 to 1.25
Outputs:
- solution_field: float32 [64, 128, 1024], P('px', 'py')
- residual: float32 [64, 128, 1024], P('px', 'py')
Inputs may be any that keep to these rules, and one draw needn't show every extreme that they name: `aggregate_id`: the cell (x, y, z) names the aggregate ((x % 4) // 2) * 2 * 128 + ((y % 8) // 4) * 128 + k of its own partition, where k differs from z // 8 by at most one; every aggregate of every partition holds cells.
All inputs are finite; a program needn't handle non-finite values.
Results may differ from a plain program's by a relative error of at most 0.0003.
Values sent between devices are 32-bit elements; how exact they have to be, the bound alone decides.
No kernel may reach another device: no remote copies, remote signals or barrier semaphores. Data moves between devices by JAX's collectives and lax.ppermute only.
A program may use at most 64 MiB of HBM per device.

v0:
```python
import jax
import jax.numpy as jnp
from jax import lax
from jax.sharding import Mesh
from jax.sharding import PartitionSpec as P

ITERS = 4
PX_PY = ("px_0", "px_1", "py_0", "py_1")
PX = ("px_0", "px_1")
PY = ("py_0", "py_1")
OMEGA = 2.0 / 3.0
FACES = (32.0, 16.0, 8.0)


def padded_2(value, sides, width):
    edges = {}
    for axis, dim in sides:
        peers, length = (lax.axis_size(axis), value.shape[dim])
        up = [(i, (i + 1) % peers) for i in range(peers - 1)]
        last = lax.slice_in_dim(value, length - width, length, axis=dim)
        first = lax.slice_in_dim(value, 0, width, axis=dim)
        edges[dim] = (
            lax.ppermute(last, axis, up),
            lax.ppermute(first, axis, [(b, a) for a, b in up]),
        )
    done = []
    for _, dim in sides:
        low, high = edges[dim]
        around = [(width, width) if d in done else (0, 0) for d in range(value.ndim)]
        value = jnp.concatenate([jnp.pad(low, around), value, jnp.pad(high, around)], axis=dim)
        done.append(dim)
    return value


def with_halo(cells, sides, width):
    for axis, dim in sides:
        count = lax.axis_size(axis)
        ends = count - 1
        head = lax.slice_in_dim(cells, 0, width, axis=dim)
        tail = lax.slice_in_dim(cells, cells.shape[dim] - width, cells.shape[dim], axis=dim)
        cells = jnp.concatenate(
            [
                lax.ppermute(tail, axis, [(i, (i + 1) % count) for i in range(ends)]),
                cells,
                lax.ppermute(head, axis, [((i + 1) % count, i) for i in range(ends)]),
            ],
            axis=dim,
        )
    return cells


def by_axis(value, axes):
    for axis in axes:
        value = lax.psum(value, axis)
    return value


def beside_sum(padded):
    padded = jnp.pad(padded, ((0, 0), (0, 0), (1, 1)))
    beside = padded[2:, 1:-1, 1:-1] + padded[:-2, 1:-1, 1:-1]
    beside = beside + padded[1:-1, 2:, 1:-1] + padded[1:-1, :-2, 1:-1]
    beside = beside + padded[1:-1, 1:-1, 2:] + padded[1:-1, 1:-1, :-2]
    return beside


def apply_fine(values, diagonal):
    widened = padded_2(values, ((PX, 0), (PY, 1)), 1)
    return (6.0 + diagonal) * values - beside_sum(widened)


def coarse_apply(coarse, coarse_diag, weights):
    weighted = weights * coarse[None]
    stacked = jnp.stack((coarse, weighted[0], weighted[1]), axis=0)
    widened = padded_2(stacked, ((PX, 1), (PY, 2)), 1)
    near = weights[0] * widened[0, 2:, 1:-1] + widened[1, :-2, 1:-1]
    near = near + weights[1] * widened[0, 1:-1, 2:] + widened[2, 1:-1, :-2]
    deep_c = jnp.pad(coarse, ((0, 0), (0, 0), (1, 1)))
    deep_w = jnp.pad(weighted[2], ((0, 0), (0, 0), (1, 1)))
    near = near + weights[2] * deep_c[:, :, 2:] + deep_w[:, :, :-2]
    return coarse_diag * coarse - near


def coarse_solve(coarse_rhs, coarse_diag, weights):
    estimate = coarse_rhs / coarse_diag
    for sweep_index in range(2):
        estimate = (
            estimate + (coarse_rhs - coarse_apply(estimate, coarse_diag, weights)) / coarse_diag
        )
    return estimate


def local(right_side, diagonal, aggregate_id, coarse_diag, coarse_link):
    rows_here = right_side.shape[0]
    cols_here = right_side.shape[1]
    depth_here = right_side.shape[2]
    rows_agg = coarse_diag.shape[0]
    cols_agg = coarse_diag.shape[1]
    depth_agg = coarse_diag.shape[2]
    scaling = 6.0 + diagonal
    faces = jnp.array(FACES, dtype=jnp.float32)
    weights = coarse_link * faces[:, None, None, None]
    home = lax.iota(jnp.int32, depth_here) // 8
    offset = aggregate_id % depth_agg - home[None, None, :]
    go_up = offset == 1
    go_down = offset == -1

    def box_sum(values):
        return values.reshape(rows_agg, 2, cols_agg, 4, depth_agg, 8).sum(axis=(1, 3, 5))

    def expand(coarse):
        wide = jnp.broadcast_to(
            coarse[:, None, :, None, :, None], (rows_agg, 2, cols_agg, 4, depth_agg, 8)
        )
        return wide.reshape(rows_here, cols_here, depth_here)

    def restrict(values):
        middle = box_sum(jnp.where(offset == 0, values, 0.0))
        upper = box_sum(jnp.where(go_up, values, 0.0))
        lower = box_sum(jnp.where(go_down, values, 0.0))
        middle = middle + jnp.pad(upper[:, :, :-1], ((0, 0), (0, 0), (1, 0)))
        return middle + jnp.pad(lower[:, :, 1:], ((0, 0), (0, 0), (0, 1)))

    def lift(coarse):
        above = jnp.pad(coarse[:, :, 1:], ((0, 0), (0, 0), (0, 1)))
        below = jnp.pad(coarse[:, :, :-1], ((0, 0), (0, 0), (1, 0)))
        return jnp.where(go_up, expand(above), jnp.where(go_down, expand(below), expand(coarse)))

    diag_wide = with_halo(diagonal, ((PX, 0), (PY, 1)), 2)
    scale_wide = 6.0 + diag_wide
    scale_mid = scale_wide[1:-1, 1:-1]
    row_global = lax.axis_index(PX) * rows_here + lax.iota(jnp.int32, rows_here + 2) - 1
    col_global = lax.axis_index(PY) * cols_here + lax.iota(jnp.int32, cols_here + 2) - 1
    row_inside = (row_global >= 0) & (row_global < rows_here * lax.axis_size(PX))
    col_inside = (col_global >= 0) & (col_global < cols_here * lax.axis_size(PY))
    inside = row_inside[:, None, None] & col_inside[None, :, None]

    def smooth_restrict(vector):
        widened = with_halo(vector, ((PX, 0), (PY, 1)), 2)
        smoothed_wide = OMEGA * widened / scale_wide
        middle = widened[1:-1, 1:-1] - (
            scale_mid * smoothed_wide[1:-1, 1:-1] - beside_sum(smoothed_wide)
        )
        middle = jnp.where(inside, middle, 0.0)
        shrunk = middle / scale_mid
        smoothed = smoothed_wide[2:-2, 2:-2]
        remainder = middle[1:-1, 1:-1]
        reduced = remainder - OMEGA * ((6.0 + diagonal) * shrunk[1:-1, 1:-1] - beside_sum(shrunk))
        return (smoothed, remainder, reduced)

    def precondition(vector):
        smoothed, remainder, reduced = smooth_restrict(vector)
        coarse_rhs = restrict(reduced)
        correction = coarse_solve(coarse_rhs, coarse_diag, weights)
        lifted = lift(correction)
        spread = lifted - OMEGA * apply_fine(lifted, diagonal) / scaling
        leftover = remainder - apply_fine(spread, diagonal)
        return smoothed + spread + OMEGA * leftover / scaling

    solution = jnp.zeros_like(right_side)
    residual = right_side
    shaped = precondition(residual)
    operated = apply_fine(shaped, diagonal)
    for iteration in range(ITERS):
        gamma_now, delta_now = (
            by_axis(jnp.sum(residual * shaped), PX_PY),
            by_axis(jnp.sum(operated * shaped), PX_PY),
        )
        further = iteration + 1 < ITERS
        if further:
            shaped_next = precondition(operated)
            applied_next = apply_fine(shaped_next, diagonal)
        if iteration == 0:
            alpha_now = gamma_now / delta_now
            direction = shaped
            along_dir = operated
            search_pre = shaped_next
            search_img = applied_next
        else:
            beta_now = gamma_now / gamma_old
            alpha_now = gamma_now / (delta_now - beta_now * gamma_now / alpha_old)
            direction = shaped + beta_now * direction
            along_dir = operated + beta_now * along_dir
            if further:
                search_pre = shaped_next + beta_now * search_pre
                search_img = applied_next + beta_now * search_img
        solution = solution + alpha_now * direction
        residual = residual - alpha_now * along_dir
        if further:
            shaped = shaped - alpha_now * search_pre
            operated = operated - alpha_now * search_img
        gamma_old = gamma_now
        alpha_old = alpha_now
    return (solution, residual)


def solution(mesh):
    finer = Mesh(mesh.devices.reshape(8, 2, 4, 4), ("px_0", "px_1", "py_0", "py_1"))
    in_specs = (
        P(PX, PY, None),
        P(PX, PY, None),
        P(PX, PY, None),
        P(PX, PY, None),
        P(None, PX, PY, None),
    )
    out_specs = (P(PX, PY, None), P(PX, PY, None))
    return jax.shard_map(local, mesh=finer, in_specs=in_specs, out_specs=out_specs, check_vma=False)
```

profile of v0, /device:TPU:8, one launch (start us, length us, event | category | flops | bytes accessed | tf_op | source)
XLA Modules:
  0.0 671.6 jit_solution(10432730826388933379)
XLA Ops:
  53.3 5.5 collective-permute-done.8
  60.8 6.0 collective-permute-start.15
  87.1 6.0 collective-permute-start.19
  95.1 5.8 collective-permute-done.18
  138.5 5.6 collective-permute-done.29
  209.1 6.0 collective-permute-start.43
  217.1 5.5 collective-permute-done.42
  240.1 5.9 collective-permute-start.49
  253.2 26.3 %all-reduce.95 = (f32[]{:T(128)}, f32[]{:T(128)}) all-reduce(f32[]{:T(128)} %get-tuple-element.9, f32[]{:T(128)} %get-tuple-element.8), channel_id=1, replica_groups=mesh['px_0'=8,'px_1'=2,'py_0'=4,'py_1'=4] {'px_0'}, use_global_device_ids=true, to_apply=%region_4.5 | all-reduce | flops 2 | bytes 16 | tf_op jit(solution)/shard_map/psum | solution.py:54
  282.6 9.8 %all-reduce.103 = (f32[]{:T(128)}, f32[]{:T(128)}) all-reduce(f32[]{:T(128)} %get-tuple-element.40, f32[]{:T(128)} %get-tuple-element.41), channel_id=1, replica_groups=mesh['px_0'=8,'px_1'=2,'py_0'=4,'py_1'=4] {'py_0'}, use_global_device_ids=true, to_apply=%region_6.7 | all-reduce | flops 2 | bytes 16 | tf_op jit(solution)/shard_map/psum | solution.py:54
  292.4 12.4 %all-reduce.99 = (f32[]{:T(128)}, f32[]{:T(128)}) all-reduce(f32[]{:T(128)} %get-tuple-element.32, f32[]{:T(128)} %get-tuple-element.33), channel_id=1, replica_groups=mesh['px_0'=8,'px_1'=2,'py_0'=4,'py_1'=4] {'py_1'}, use_global_device_ids=true, to_apply=%region_7.8 | all-reduce | flops 2 | bytes 16 | tf_op jit(solution)/shard_map/psum | solution.py:54
  376.7 6.0 collective-permute-start.67
  384.7 5.8 collective-permute-done.66
  416.5 25.0 %all-reduce.94 = (f32[]{:T(128)}, f32[]{:T(128)}) all-reduce(f32[]{:T(128)} %get-tuple-element.7, f32[]{:T(128)} %get-tuple-element.6), channel_id=1, replica_groups=mesh['px_0'=8,'px_1'=2,'py_0'=4,'py_1'=4] {'px_0'}, use_global_device_ids=true, to_apply=%region_17.18 | all-reduce | flops 2 | bytes 16 | tf_op jit(solution)/shard_map/psum | solution.py:54
  444.6 8.6 %all-reduce.102 = (f32[]{:T(128)}, f32[]{:T(128)}) all-reduce(f32[]{:T(128)} %get-tuple-element.38, f32[]{:T(128)} %get-tuple-element.39), channel_id=1, replica_groups=mesh['px_0'=8,'px_1'=2,'py_0'=4,'py_1'=4] {'py_0'}, use_global_device_ids=true, to_apply=%region_19.20 | all-reduce | flops 2 | bytes 16 | tf_op jit(solution)/shard_map/psum | solution.py:54
  453.3 12.3 %all-reduce.98 = (f32[]{:T(128)}, f32[]{:T(128)}) all-reduce(f32[]{:T(128)} %get-tuple-element.30, f32[]{:T(128)} %get-tuple-element.31), channel_id=1, replica_groups=mesh['px_0'=8,'px_1'=2,'py_0'=4,'py_1'=4] {'py_1'}, use_global_device_ids=true, to_apply=%region_20.21 | all-reduce | flops 2 | bytes 16 | tf_op jit(solution)/shard_map/psum | solution.py:54
  532.3 6.0 collective-permute-start.91
  540.3 5.8 collective-permute-done.90
  572.1 25.0 %all-reduce.93 = (f32[]{:T(128)}, f32[]{:T(128)}) all-reduce(f32[]{:T(128)} %get-tuple-element.5, f32[]{:T(128)} %get-tuple-element.4), channel_id=1, replica_groups=mesh['px_0'=8,'px_1'=2,'py_0'=4,'py_1'=4] {'px_0'}, use_global_device_ids=true, to_apply=%region_30.31 | all-reduce | flops 2 | bytes 16 | tf_op jit(solution)/shard_map/psum | solution.py:54
  600.2 8.3 %all-reduce.101 = (f32[]{:T(128)}, f32[]{:T(128)}) all-reduce(f32[]{:T(128)} %get-tuple-element.36, f32[]{:T(128)} %get-tuple-element.37), channel_id=1, replica_groups=mesh['px_0'=8,'px_1'=2,'py_0'=4,'py_1'=4] {'py_0'}, use_global_device_ids=true, to_apply=%region_32.33 | all-reduce | flops 2 | bytes 16 | tf_op jit(solution)/shard_map/psum | solution.py:54
  608.5 12.6 %all-reduce.97 = (f32[]{:T(128)}, f32[]{:T(128)}) all-reduce(f32[]{:T(128)} %get-tuple-element.28, f32[]{:T(128)} %get-tuple-element.29), channel_id=1, replica_groups=mesh['px_0'=8,'px_1'=2,'py_0'=4,'py_1'=4] {'py_1'}, use_global_device_ids=true, to_apply=%region_33.34 | all-reduce | flops 2 | bytes 16 | tf_op jit(solution)/shard_map/psum | solution.py:54
  626.2 18.0 %all-reduce.92 = (f32[]{:T(128)}, f32[]{:T(128)}) all-reduce(f32[]{:T(128)} %get-tuple-element.3, f32[]{:T(128)} %get-tuple-element.2), channel_id=1, replica_groups=mesh['px_0'=8,'px_1'=2,'py_0'=4,'py_1'=4] {'px_0'}, use_global_device_ids=true, to_apply=%region_43.44 | all-reduce | flops 2 | bytes 16 | tf_op jit(solution)/shard_map/psum | solution.py:54
  647.3 8.3 %all-reduce.100 = (f32[]{:T(128)}, f32[]{:T(128)}) all-reduce(f32[]{:T(128)} %get-tuple-element.34, f32[]{:T(128)} %get-tuple-element.35), channel_id=1, replica_groups=mesh['px_0'=8,'px_1'=2,'py_0'=4,'py_1'=4] {'py_0'}, use_global_device_ids=true, to_apply=%region_45.46 | all-reduce | flops 2 | bytes 16 | tf_op jit(solution)/shard_map/psum | solution.py:54
  655.7 10.9 %all-reduce.96 = (f32[]{:T(128)}, f32[]{:T(128)}) all-reduce(f32[]{:T(128)} %get-tuple-element.26, f32[]{:T(128)} %get-tuple-element.27), channel_id=1, replica_groups=mesh['px_0'=8,'px_1'=2,'py_0'=4,'py_1'=4] {'py_1'}, use_global_device_ids=true, to_apply=%region_46.47 | all-reduce | flops 2 | bytes 16 | tf_op jit(solution)/shard_map/psum | solution.py:54
  (523 shorter events, 406.8 us)
Async XLA Ops:
  1.5 19.3 %collective-permute-start.1 = (f32[2,8,1024]{2,1,0:T(8,128)S(1)}, f32[2,8,1024]{2,1,0:T(8,128)S(1)}, u32[]{:S(2)}, u32[]{:S(2)}) collective-permute-start(f32[2,8,1024]{2,1,0:T(8,128)S(1)} %get-tuple-element.165), channel_id=1, source_target_pairs={{16,0},{32,16},{48,32},{64,48},{80,64},{96,80},{112,96},{128,112},... | collective-permute-start | bytes 196616 | tf_op jit(solution)/shard_map/ppermute | solution.py:45
  2.8 17.1 %collective-permute-start = (f32[2,8,1024]{2,1,0:T(8,128)S(1)}, f32[2,8,1024]{2,1,0:T(8,128)S(1)}, u32[]{:S(2)}, u32[]{:S(2)}) collective-permute-start(f32[2,8,1024]{2,1,0:T(8,128)S(1)} %get-tuple-element.166), channel_id=1, source_target_pairs={{0,16},{16,32},{32,48},{48,64},{64,80},{80,96},{96,112},{112,128},... | collective-permute-start | bytes 196616 | tf_op jit(solution)/shard_map/ppermute | solution.py:43
  81.7 19.3 %collective-permute-start.17 = (f32[1,8,1024]{2,1,0:T(8,128)S(1)}, f32[1,8,1024]{2,1,0:T(8,128)S(1)}, u32[]{:S(2)}, u32[]{:S(2)}) collective-permute-start(f32[1,8,1024]{2,1,0:T(8,128)S(1)} %get-tuple-element.161), channel_id=1, source_target_pairs={{0,16},{16,32},{32,48},{48,64},{64,80},{80,96},{96,112},{112,128},... | collective-permute-start | bytes 98312 | tf_op jit(solution)/shard_map/ppermute | solution.py:23
  85.8 15.2 %collective-permute-start.16 = (f32[1,8,1024]{2,1,0:T(8,128)S(1)}, f32[1,8,1024]{2,1,0:T(8,128)S(1)}, u32[]{:S(2)}, u32[]{:S(2)}) collective-permute-start(f32[1,8,1024]{2,1,0:T(8,128)S(1)} %get-tuple-element.162), channel_id=1, source_target_pairs={{16,0},{32,16},{48,32},{64,48},{80,64},{96,80},{112,96},{128,112},... | collective-permute-start | bytes 98312 | tf_op jit(solution)/shard_map/ppermute | solution.py:24
  116.0 15.3 %collective-permute-start.25 = (f32[1,8,1024]{2,1,0:T(8,128)S(1)}, f32[1,8,1024]{2,1,0:T(8,128)S(1)}, u32[]{:S(2)}, u32[]{:S(2)}) collective-permute-start(f32[1,8,1024]{2,1,0:T(8,128)S(1)} %get-tuple-element.153), channel_id=1, source_target_pairs={{0,16},{16,32},{32,48},{48,64},{64,80},{80,96},{96,112},{112,128},... | collective-permute-start | bytes 98312 | tf_op jit(solution)/shard_map/ppermute | solution.py:23
  203.2 19.5 %collective-permute-start.41 = (f32[1,8,1024]{2,1,0:T(8,128)S(1)}, f32[1,8,1024]{2,1,0:T(8,128)S(1)}, u32[]{:S(2)}, u32[]{:S(2)}) collective-permute-start(f32[1,8,1024]{2,1,0:T(8,128)S(1)} %get-tuple-element.145), channel_id=1, source_target_pairs={{0,16},{16,32},{32,48},{48,64},{64,80},{80,96},{96,112},{112,128},... | collective-permute-start | bytes 98312 | tf_op jit(solution)/shard_map/ppermute | solution.py:23
  207.8 14.9 %collective-permute-start.40 = (f32[1,8,1024]{2,1,0:T(8,128)S(1)}, f32[1,8,1024]{2,1,0:T(8,128)S(1)}, u32[]{:S(2)}, u32[]{:S(2)}) collective-permute-start(f32[1,8,1024]{2,1,0:T(8,128)S(1)} %get-tuple-element.146), channel_id=1, source_target_pairs={{16,0},{32,16},{48,32},{64,48},{80,64},{96,80},{112,96},{128,112},... | collective-permute-start | bytes 98312 | tf_op jit(solution)/shard_map/ppermute | solution.py:24
  223.1 15.4 %collective-permute-start.45 = (f32[1,8,1024]{2,1,0:T(8,128)S(1)}, f32[1,8,1024]{2,1,0:T(8,128)S(1)}, u32[]{:S(2)}, u32[]{:S(2)}) collective-permute-start(f32[1,8,1024]{2,1,0:T(8,128)S(1)} %get-tuple-element.141), channel_id=1, source_target_pairs={{0,16},{16,32},{32,48},{48,64},{64,80},{80,96},{96,112},{112,128},... | collective-permute-start | bytes 98312 | tf_op jit(solution)/shard_map/ppermute | solution.py:23
  240.1 66.1 %collective-permute-start.49 = (f32[1,8,1024]{2,1,0:T(8,128)S(1)}, f32[1,8,1024]{2,1,0:T(8,128)S(1)}, u32[]{:S(2)}, u32[]{:S(2)}) collective-permute-start(f32[1,8,1024]{2,1,0:T(8,128)S(1)} %get-tuple-element.137), channel_id=1, source_target_pairs={{0,16},{16,32},{32,48},{48,64},{64,80},{80,96},{96,112},{112,128},... | collective-permute-start | bytes 98312 | tf_op jit(solution)/shard_map/ppermute | solution.py:23
  246.0 60.1 %collective-permute-start.48 = (f32[1,8,1024]{2,1,0:T(8,128)S(1)}, f32[1,8,1024]{2,1,0:T(8,128)S(1)}, u32[]{:S(2)}, u32[]{:S(2)}) collective-permute-start(f32[1,8,1024]{2,1,0:T(8,128)S(1)} %get-tuple-element.138), channel_id=1, source_target_pairs={{16,0},{32,16},{48,32},{64,48},{80,64},{96,80},{112,96},{128,112},... | collective-permute-start | bytes 98312 | tf_op jit(solution)/shard_map/ppermute | solution.py:24
  247.4 58.7 %collective-permute-start.51 = (f32[4,1,1024]{2,1,0:T(1,128)S(1)}, f32[4,1,1024]{2,1,0:T(1,128)S(1)}, u32[]{:S(2)}, u32[]{:S(2)}) collective-permute-start(f32[4,1,1024]{2,1,0:T(1,128)S(1)} %get-tuple-element.139), channel_id=1, source_target_pairs={{0,1},{1,2},{2,3},{3,4},{4,5},{5,6},{6,7},{7,8},{8,9},{9,10},{10,1... | collective-permute-start | bytes 49160 | tf_op jit(solution)/shard_map/ppermute | solution.py:23
  251.0 55.1 %collective-permute-start.50 = (f32[4,1,1024]{2,1,0:T(1,128)S(1)}, f32[4,1,1024]{2,1,0:T(1,128)S(1)}, u32[]{:S(2)}, u32[]{:S(2)}) collective-permute-start(f32[4,1,1024]{2,1,0:T(1,128)S(1)} %get-tuple-element.140), channel_id=1, source_target_pairs={{1,0},{2,1},{3,2},{4,3},{5,4},{6,5},{7,6},{8,7},{9,8},{10,9},{11,1... | collective-permute-start | bytes 49160 | tf_op jit(solution)/shard_map/ppermute | solution.py:24
  371.3 19.3 %collective-permute-start.65 = (f32[1,8,1024]{2,1,0:T(8,128)S(1)}, f32[1,8,1024]{2,1,0:T(8,128)S(1)}, u32[]{:S(2)}, u32[]{:S(2)}) collective-permute-start(f32[1,8,1024]{2,1,0:T(8,128)S(1)} %get-tuple-element.129), channel_id=1, source_target_pairs={{0,16},{16,32},{32,48},{48,64},{64,80},{80,96},{96,112},{112,128},... | collective-permute-start | bytes 98312 | tf_op jit(solution)/shard_map/ppermute | solution.py:23
  375.4 15.2 %collective-permute-start.64 = (f32[1,8,1024]{2,1,0:T(8,128)S(1)}, f32[1,8,1024]{2,1,0:T(8,128)S(1)}, u32[]{:S(2)}, u32[]{:S(2)}) collective-permute-start(f32[1,8,1024]{2,1,0:T(8,128)S(1)} %get-tuple-element.130), channel_id=1, source_target_pairs={{16,0},{32,16},{48,32},{64,48},{80,64},{96,80},{112,96},{128,112},... | collective-permute-start | bytes 98312 | tf_op jit(solution)/shard_map/ppermute | solution.py:24
  405.7 64.3 %collective-permute-start.73 = (f32[1,8,1024]{2,1,0:T(8,128)S(1)}, f32[1,8,1024]{2,1,0:T(8,128)S(1)}, u32[]{:S(2)}, u32[]{:S(2)}) collective-permute-start(f32[1,8,1024]{2,1,0:T(8,128)S(1)} %get-tuple-element.121), channel_id=1, source_target_pairs={{0,16},{16,32},{32,48},{48,64},{64,80},{80,96},{96,112},{112,128},... | collective-permute-start | bytes 98312 | tf_op jit(solution)/shard_map/ppermute | solution.py:23
  409.3 60.6 %collective-permute-start.72 = (f32[1,8,1024]{2,1,0:T(8,128)S(1)}, f32[1,8,1024]{2,1,0:T(8,128)S(1)}, u32[]{:S(2)}, u32[]{:S(2)}) collective-permute-start(f32[1,8,1024]{2,1,0:T(8,128)S(1)} %get-tuple-element.122), channel_id=1, source_target_pairs={{16,0},{32,16},{48,32},{64,48},{80,64},{96,80},{112,96},{128,112},... | collective-permute-start | bytes 98312 | tf_op jit(solution)/shard_map/ppermute | solution.py:24
  410.7 59.2 %collective-permute-start.75 = (f32[4,1,1024]{2,1,0:T(1,128)S(1)}, f32[4,1,1024]{2,1,0:T(1,128)S(1)}, u32[]{:S(2)}, u32[]{:S(2)}) collective-permute-start(f32[4,1,1024]{2,1,0:T(1,128)S(1)} %get-tuple-element.123), channel_id=1, source_target_pairs={{0,1},{1,2},{2,3},{3,4},{4,5},{5,6},{6,7},{7,8},{8,9},{9,10},{10,1... | collective-permute-start | bytes 49160 | tf_op jit(solution)/shard_map/ppermute | solution.py:23
  414.3 55.6 %collective-permute-start.74 = (f32[4,1,1024]{2,1,0:T(1,128)S(1)}, f32[4,1,1024]{2,1,0:T(1,128)S(1)}, u32[]{:S(2)}, u32[]{:S(2)}) collective-permute-start(f32[4,1,1024]{2,1,0:T(1,128)S(1)} %get-tuple-element.124), channel_id=1, source_target_pairs={{1,0},{2,1},{3,2},{4,3},{5,4},{6,5},{7,6},{8,7},{9,8},{10,9},{11,1... | collective-permute-start | bytes 49160 | tf_op jit(solution)/shard_map/ppermute | solution.py:24
  526.9 19.3 %collective-permute-start.89 = (f32[1,8,1024]{2,1,0:T(8,128)S(1)}, f32[1,8,1024]{2,1,0:T(8,128)S(1)}, u32[]{:S(2)}, u32[]{:S(2)}) collective-permute-start(f32[1,8,1024]{2,1,0:T(8,128)S(1)} %get-tuple-element.113), channel_id=1, source_target_pairs={{0,16},{16,32},{32,48},{48,64},{64,80},{80,96},{96,112},{112,128},... | collective-permute-start | bytes 98312 | tf_op jit(solution)/shard_map/ppermute | solution.py:23
  531.0 15.2 %collective-permute-start.88 = (f32[1,8,1024]{2,1,0:T(8,128)S(1)}, f32[1,8,1024]{2,1,0:T(8,128)S(1)}, u32[]{:S(2)}, u32[]{:S(2)}) collective-permute-start(f32[1,8,1024]{2,1,0:T(8,128)S(1)} %get-tuple-element.114), channel_id=1, source_target_pairs={{16,0},{32,16},{48,32},{64,48},{80,64},{96,80},{112,96},{128,112},... | collective-permute-start | bytes 98312 | tf_op jit(solution)/shard_map/ppermute | solution.py:24
  561.2 63.8 %collective-permute-start.97 = (f32[1,8,1024]{2,1,0:T(8,128)S(1)}, f32[1,8,1024]{2,1,0:T(8,128)S(1)}, u32[]{:S(2)}, u32[]{:S(2)}) collective-permute-start(f32[1,8,1024]{2,1,0:T(8,128)S(1)} %get-tuple-element.105), channel_id=1, source_target_pairs={{0,16},{16,32},{32,48},{48,64},{64,80},{80,96},{96,112},{112,128},... | collective-permute-start | bytes 98312 | tf_op jit(solution)/shard_map/ppermute | solution.py:23
  564.9 60.1 %collective-permute-start.96 = (f32[1,8,1024]{2,1,0:T(8,128)S(1)}, f32[1,8,1024]{2,1,0:T(8,128)S(1)}, u32[]{:S(2)}, u32[]{:S(2)}) collective-permute-start(f32[1,8,1024]{2,1,0:T(8,128)S(1)} %get-tuple-element.106), channel_id=1, source_target_pairs={{16,0},{32,16},{48,32},{64,48},{80,64},{96,80},{112,96},{128,112},... | collective-permute-start | bytes 98312 | tf_op jit(solution)/shard_map/ppermute | solution.py:24
  566.2 58.7 %collective-permute-start.99 = (f32[4,1,1024]{2,1,0:T(1,128)S(1)}, f32[4,1,1024]{2,1,0:T(1,128)S(1)}, u32[]{:S(2)}, u32[]{:S(2)}) collective-permute-start(f32[4,1,1024]{2,1,0:T(1,128)S(1)} %get-tuple-element.107), channel_id=1, source_target_pairs={{0,1},{1,2},{2,3},{3,4},{4,5},{5,6},{6,7},{7,8},{8,9},{9,10},{10,1... | collective-permute-start | bytes 49160 | tf_op jit(solution)/shard_map/ppermute | solution.py:23
  569.9 55.1 %collective-permute-start.98 = (f32[4,1,1024]{2,1,0:T(1,128)S(1)}, f32[4,1,1024]{2,1,0:T(1,128)S(1)}, u32[]{:S(2)}, u32[]{:S(2)}) collective-permute-start(f32[4,1,1024]{2,1,0:T(1,128)S(1)} %get-tuple-element.108), channel_id=1, source_target_pairs={{1,0},{2,1},{3,2},{4,3},{5,4},{6,5},{7,6},{8,7},{9,8},{10,9},{11,1... | collective-permute-start | bytes 49160 | tf_op jit(solution)/shard_map/ppermute | solution.py:24
  (127 other events, 3584.0 us)
where the time goes:
time: 684 us; the launch traced here: 672 us
  starting transfers between devices  281 us (41%)
  blocking collectives  190 us (28%)
  waiting for transfers between devices  93.3 us (14%)
  local copies, waits for them, and re-layouts  55.5 us (8%)
  other arithmetic  34.7 us (5%)
  between operations  17.3 us (3%)
    psum x16, blocking collectives, by_axis(): value = lax.psum(value, axis)  190 us
    ppermute x40, starting transfers between devices, padded_2(): lax.ppermute(last, axis, up)  157 us
    ppermute x40, starting transfers between devices, padded_2(): lax.ppermute(first, axis, [(b, a) for a, b in up])  73.7 us
    ppermute x40, waiting for transfers between devices, padded_2(): lax.ppermute(first, axis, [(b, a) for a, b in up])  66.1 us
    ppermute x10, starting transfers between devices, with_halo(): lax.ppermute(tail, axis, [(i, (i + 1) % count) for i in range(ends)])  28.7 us
    ppermute x10, waiting for transfers between devices, with_halo(): lax.ppermute(head, axis, [((i + 1) % count, i) for i in range(ends)])  25.5 us
    reshape x12, local copies, waits for them, and re-layouts, box_sum(): values.reshape(rows_agg, 2, cols_agg, 4, depth_agg, 8).sum(axis=(1, 3, 5))  22.2 us
    ppermute x10, starting transfers between devices, with_halo(): lax.ppermute(head, axis, [((i + 1) % count, i) for i in range(ends)])  21.8 us
  transfers between devices with their start and end apart: 100, of which 29 were waited for; matrix products, arithmetic and copies ran while one was open for 1% of the time, Pallas kernels for 0%

commit v1 on v0

--- a/solution.py
+++ b/solution.py
@@ -51,7 +51,7 @@
 
 def by_axis(value, axes):
     for axis in axes:
-        value = lax.psum(value, axis)
+        value = jnp.sum(lax.all_gather(value, axis), axis=0)
     return value
 
 

time: 684 us -> 737 us (1.077)
  local copies, waits for them, and re-layouts: 55.5 us -> 106 us
  waiting for transfers between devices: 93.3 us -> 43.4 us
  starting transfers between devices: 281 us -> 316 us
  other arithmetic: 34.7 us -> 56.5 us
    psum x16 -> x0, blocking collectives: 190 us -> none  [by_axis(): value = lax.psum(value, axis)]
    unnamed x0 -> x16, blocking collectives: none -> 184 us
    ppermute x40, waiting for transfers between devices: 66.1 us -> 0.11 us  [padded_2(): lax.ppermute(first, axis, [(b, a) for a, b in up])]
    unnamed x106 -> x188, local copies, waits for them, and re-layouts: 3.48 us -> 49.6 us
    ppermute x40, starting transfers between devices: 157 us -> 195 us  [padded_2(): lax.ppermute(last, axis, up)]
    reduce_sum x0 -> x32, other arithmetic: none -> 20.1 us  [by_axis(): value = jnp.sum(lax.all_gather(value, axis), axis=0)]
    ppermute x40, waiting for transfers between devices: 0.11 us -> 18.6 us  [padded_2(): lax.ppermute(last, axis, up)]
  transfers between devices with their start and end apart: 100 -> 100, of which waited for: 29 -> 27; matrix products, arithmetic and copies ran while one was open for 1% -> 7% of each run, Pallas kernels for 0% -> 0%
where the time goes in v1:
time: 737 us; the launch traced here: 724 us
  starting transfers between devices  316 us (43%)
  blocking collectives  184 us (25%)
  local copies, waits for them, and re-layouts  106 us (14%)
  other arithmetic  56.5 us (8%)
  waiting for transfers between devices  43.4 us (6%)
  between operations  17.6 us (2%)
    ppermute x40, starting transfers between devices, padded_2(): lax.ppermute(last, axis, up)  195 us
    unnamed x16, blocking collectives  184 us
    ppermute x40, starting transfers between devices, padded_2(): lax.ppermute(first, axis, [(b, a) for a, b in up])  71.9 us
    unnamed x188, local copies, waits for them, and re-layouts  49.6 us
    ppermute x10, starting transfers between devices, with_halo(): lax.ppermute(tail, axis, [(i, (i + 1) % count) for i in range(ends)])  28.9 us
    reshape x12, local copies, waits for them, and re-layouts, box_sum(): values.reshape(rows_agg, 2, cols_agg, 4, depth_agg, 8).sum(axis=(1, 3, 5))  26.2 us
    ppermute x10, waiting for transfers between devices, with_halo(): lax.ppermute(head, axis, [((i + 1) % count, i) for i in range(ends)])  23.8 us
    ppermute x10, starting transfers between devices, with_halo(): lax.ppermute(head, axis, [((i + 1) % count, i) for i in range(ends)])  21.1 us
  transfers between devices with their start and end apart: 100, of which 27 were waited for; matrix products, arithmetic and copies ran while one was open for 7% of the time, Pallas kernels for 0%

profile of v1, /device:TPU:8, one launch (start us, length us, event | category | flops | bytes accessed | tf_op | source)
XLA Modules:
  0.0 723.6 jit_solution(8175337163140676275)
XLA Ops:
  54.7 6.1 collective-permute-start.15
  85.1 6.0 collective-permute-start.19
  100.3 6.0 collective-permute-start.23
  131.1 6.2 collective-permute-start.30
  139.3 6.4 collective-permute-done.31
  159.8 6.3 collective-permute-start.35
  181.3 7.0 collective-permute-start.37
  205.2 6.0 collective-permute-start.43
  238.0 6.0 collective-permute-start.51
  248.0 25.1 %all-reduce.127 = (f32[8]{0:T(128)S(1)}, f32[8]{0:T(128)S(1)}) all-reduce(f32[8]{0:T(128)S(1)} %dynamic-update-slice, f32[8]{0:T(128)S(1)} %dynamic-update-slice.4), channel_id=1, replica_groups=mesh['px_0'=8,'px_1'=2,'py_0'=4,'py_1'=4] {'px_0'}, use_global_device_ids=true, to_apply=%add.92 | all-reduce | flops 16 | bytes 128
  284.6 15.3 %all-reduce.135 = (f32[4]{0:T(128)S(1)}, f32[4]{0:T(128)S(1)}) all-reduce(f32[4]{0:T(128)S(1)} %dynamic-update-slice.2, f32[4]{0:T(128)S(1)} %dynamic-update-slice.6), channel_id=1, replica_groups=mesh['px_0'=8,'px_1'=2,'py_0'=4,'py_1'=4] {'py_0'}, use_global_device_ids=true, to_apply=%add.94 | all-reduce | flops 8 | bytes 64
  303.8 9.7 %all-reduce.131 = (f32[4]{0:T(128)S(1)}, f32[4]{0:T(128)S(1)}) all-reduce(f32[4]{0:T(128)S(1)} %dynamic-update-slice.3, f32[4]{0:T(128)S(1)} %dynamic-update-slice.7), channel_id=1, replica_groups=mesh['px_0'=8,'px_1'=2,'py_0'=4,'py_1'=4] {'py_1'}, use_global_device_ids=true, to_apply=%add.95 | all-reduce | flops 8 | bytes 64
  405.3 6.0 collective-permute-start.71
  430.0 21.0 %all-reduce.126 = (f32[8]{0:T(128)S(1)}, f32[8]{0:T(128)S(1)}) all-reduce(f32[8]{0:T(128)S(1)} %dynamic-update-slice.8, f32[8]{0:T(128)S(1)} %dynamic-update-slice.12), channel_id=1, replica_groups=mesh['px_0'=8,'px_1'=2,'py_0'=4,'py_1'=4] {'px_0'}, use_global_device_ids=true, to_apply=%add.100 | all-reduce | flops 16 | bytes 128
  461.1 13.9 %all-reduce.134 = (f32[4]{0:T(128)S(1)}, f32[4]{0:T(128)S(1)}) all-reduce(f32[4]{0:T(128)S(1)} %dynamic-update-slice.10, f32[4]{0:T(128)S(1)} %dynamic-update-slice.14), channel_id=1, replica_groups=mesh['px_0'=8,'px_1'=2,'py_0'=4,'py_1'=4] {'py_0'}, use_global_device_ids=true, to_apply=%add.102 | all-reduce | flops 8 | bytes 64
  478.7 9.7 %all-reduce.130 = (f32[4]{0:T(128)S(1)}, f32[4]{0:T(128)S(1)}) all-reduce(f32[4]{0:T(128)S(1)} %dynamic-update-slice.11, f32[4]{0:T(128)S(1)} %dynamic-update-slice.15), channel_id=1, replica_groups=mesh['px_0'=8,'px_1'=2,'py_0'=4,'py_1'=4] {'py_1'}, use_global_device_ids=true, to_apply=%add.103 | all-reduce | flops 8 | bytes 64
  559.5 6.0 collective-permute-start.91
  575.1 6.0 collective-permute-start.95
  599.3 21.0 %all-reduce.125 = (f32[8]{0:T(128)S(1)}, f32[8]{0:T(128)S(1)}) all-reduce(f32[8]{0:T(128)S(1)} %dynamic-update-slice.16, f32[8]{0:T(128)S(1)} %dynamic-update-slice.20), channel_id=1, replica_groups=mesh['px_0'=8,'px_1'=2,'py_0'=4,'py_1'=4] {'px_0'}, use_global_device_ids=true, to_apply=%add.108 | all-reduce | flops 16 | bytes 128
  631.1 13.9 %all-reduce.133 = (f32[4]{0:T(128)S(1)}, f32[4]{0:T(128)S(1)}) all-reduce(f32[4]{0:T(128)S(1)} %dynamic-update-slice.18, f32[4]{0:T(128)S(1)} %dynamic-update-slice.22), channel_id=1, replica_groups=mesh['px_0'=8,'px_1'=2,'py_0'=4,'py_1'=4] {'py_0'}, use_global_device_ids=true, to_apply=%add.110 | all-reduce | flops 8 | bytes 64
  649.1 9.7 %all-reduce.129 = (f32[4]{0:T(128)S(1)}, f32[4]{0:T(128)S(1)}) all-reduce(f32[4]{0:T(128)S(1)} %dynamic-update-slice.19, f32[4]{0:T(128)S(1)} %dynamic-update-slice.23), channel_id=1, replica_groups=mesh['px_0'=8,'px_1'=2,'py_0'=4,'py_1'=4] {'py_1'}, use_global_device_ids=true, to_apply=%add.111 | all-reduce | flops 8 | bytes 64
  668.1 17.0 %all-reduce.124 = (f32[8]{0:T(128)S(1)}, f32[8]{0:T(128)S(1)}) all-reduce(f32[8]{0:T(128)S(1)} %dynamic-update-slice.24, f32[8]{0:T(128)S(1)} %dynamic-update-slice.28), channel_id=1, replica_groups=mesh['px_0'=8,'px_1'=2,'py_0'=4,'py_1'=4] {'px_0'}, use_global_device_ids=true, to_apply=%add.116 | all-reduce | flops 16 | bytes 128
  695.4 7.7 %all-reduce.132 = (f32[4]{0:T(128)S(1)}, f32[4]{0:T(128)S(1)}) all-reduce(f32[4]{0:T(128)S(1)} %dynamic-update-slice.26, f32[4]{0:T(128)S(1)} %dynamic-update-slice.30), channel_id=1, replica_groups=mesh['px_0'=8,'px_1'=2,'py_0'=4,'py_1'=4] {'py_0'}, use_global_device_ids=true, to_apply=%add.118 | all-reduce | flops 8 | bytes 64
  707.0 10.4 %all-reduce.128 = (f32[4]{0:T(128)S(1)}, f32[4]{0:T(128)S(1)}) all-reduce(f32[4]{0:T(128)S(1)} %dynamic-update-slice.27, f32[4]{0:T(128)S(1)} %dynamic-update-slice.31), channel_id=1, replica_groups=mesh['px_0'=8,'px_1'=2,'py_0'=4,'py_1'=4] {'py_1'}, use_global_device_ids=true, to_apply=%add.119 | all-reduce | flops 8 | bytes 64
  (637 shorter events, 457.4 us)
Async XLA Ops:
  52.7 15.1 %collective-permute-start.14 = (f32[3,2,1,128]{3,2,1,0:T(1,128)S(1)}, f32[3,2,1,128]{3,2,1,0:T(1,128)S(1)}, u32[]{:S(2)}, u32[]{:S(2)}) collective-permute-start(f32[3,2,1,128]{3,2,1,0:T(1,128)S(1)} %get-tuple-element.193), channel_id=1, source_target_pairs={{1,0},{2,1},{3,2},{4,3},{5,4},{6,5},{7,6},{8,7},{9,8},{10,9},{11,1... | collective-permute-start | bytes 9224 | tf_op jit(solution)/shard_map/ppermute | solution.py:24
  76.8 15.8 %collective-permute-start.16 = (f32[1,8,1024]{2,1,0:T(8,128)S(1)}, f32[1,8,1024]{2,1,0:T(8,128)S(1)}, u32[]{:S(2)}, u32[]{:S(2)}) collective-permute-start(f32[1,8,1024]{2,1,0:T(8,128)S(1)} %get-tuple-element.162), channel_id=1, source_target_pairs={{16,0},{32,16},{48,32},{64,48},{80,64},{96,80},{112,96},{128,112},... | collective-permute-start | bytes 98312 | tf_op jit(solution)/shard_map/ppermute | solution.py:24
  78.1 14.5 %collective-permute-start.17 = (f32[1,8,1024]{2,1,0:T(8,128)S(1)}, f32[1,8,1024]{2,1,0:T(8,128)S(1)}, u32[]{:S(2)}, u32[]{:S(2)}) collective-permute-start(f32[1,8,1024]{2,1,0:T(8,128)S(1)} %get-tuple-element.161), channel_id=1, source_target_pairs={{0,16},{16,32},{32,48},{48,64},{64,80},{80,96},{96,112},{112,128},... | collective-permute-start | bytes 98312 | tf_op jit(solution)/shard_map/ppermute | solution.py:23
  93.1 14.7 %collective-permute-start.20 = (f32[1,8,1024]{2,1,0:T(8,128)S(1)}, f32[1,8,1024]{2,1,0:T(8,128)S(1)}, u32[]{:S(2)}, u32[]{:S(2)}) collective-permute-start(f32[1,8,1024]{2,1,0:T(8,128)S(1)} %get-tuple-element.158), channel_id=1, source_target_pairs={{16,0},{32,16},{48,32},{64,48},{80,64},{96,80},{112,96},{128,112},... | collective-permute-start | bytes 98312 | tf_op jit(solution)/shard_map/ppermute | solution.py:24
  172.3 16.0 %collective-permute-start.38 = (f32[3,2,1,128]{3,2,1,0:T(1,128)S(1)}, f32[3,2,1,128]{3,2,1,0:T(1,128)S(1)}, u32[]{:S(2)}, u32[]{:S(2)}) collective-permute-start(f32[3,2,1,128]{3,2,1,0:T(1,128)S(1)} %get-tuple-element.185), channel_id=1, source_target_pairs={{1,0},{2,1},{3,2},{4,3},{5,4},{6,5},{7,6},{8,7},{9,8},{10,9},{11,1... | collective-permute-start | bytes 9224 | tf_op jit(solution)/shard_map/ppermute | solution.py:24
  197.0 15.8 %collective-permute-start.40 = (f32[1,8,1024]{2,1,0:T(8,128)S(1)}, f32[1,8,1024]{2,1,0:T(8,128)S(1)}, u32[]{:S(2)}, u32[]{:S(2)}) collective-permute-start(f32[1,8,1024]{2,1,0:T(8,128)S(1)} %get-tuple-element.146), channel_id=1, source_target_pairs={{16,0},{32,16},{48,32},{64,48},{80,64},{96,80},{112,96},{128,112},... | collective-permute-start | bytes 98312 | tf_op jit(solution)/shard_map/ppermute | solution.py:24
  198.3 14.5 %collective-permute-start.41 = (f32[1,8,1024]{2,1,0:T(8,128)S(1)}, f32[1,8,1024]{2,1,0:T(8,128)S(1)}, u32[]{:S(2)}, u32[]{:S(2)}) collective-permute-start(f32[1,8,1024]{2,1,0:T(8,128)S(1)} %get-tuple-element.145), channel_id=1, source_target_pairs={{0,16},{16,32},{32,48},{48,64},{64,80},{80,96},{96,112},{112,128},... | collective-permute-start | bytes 98312 | tf_op jit(solution)/shard_map/ppermute | solution.py:23
  213.2 14.7 %collective-permute-start.44 = (f32[1,8,1024]{2,1,0:T(8,128)S(1)}, f32[1,8,1024]{2,1,0:T(8,128)S(1)}, u32[]{:S(2)}, u32[]{:S(2)}) collective-permute-start(f32[1,8,1024]{2,1,0:T(8,128)S(1)} %get-tuple-element.142), channel_id=1, source_target_pairs={{16,0},{32,16},{48,32},{64,48},{80,64},{96,80},{112,96},{128,112},... | collective-permute-start | bytes 98312 | tf_op jit(solution)/shard_map/ppermute | solution.py:24
  229.5 86.7 %collective-permute-start.48 = (f32[1,8,1024]{2,1,0:T(8,128)S(1)}, f32[1,8,1024]{2,1,0:T(8,128)S(1)}, u32[]{:S(2)}, u32[]{:S(2)}) collective-permute-start(f32[1,8,1024]{2,1,0:T(8,128)S(1)} %get-tuple-element.138), channel_id=1, source_target_pairs={{16,0},{32,16},{48,32},{64,48},{80,64},{96,80},{112,96},{128,112},... | collective-permute-start | bytes 98312 | tf_op jit(solution)/shard_map/ppermute | solution.py:24
  230.8 85.4 %collective-permute-start.49 = (f32[1,8,1024]{2,1,0:T(8,128)S(1)}, f32[1,8,1024]{2,1,0:T(8,128)S(1)}, u32[]{:S(2)}, u32[]{:S(2)}) collective-permute-start(f32[1,8,1024]{2,1,0:T(8,128)S(1)} %get-tuple-element.137), channel_id=1, source_target_pairs={{0,16},{16,32},{32,48},{48,64},{64,80},{80,96},{96,112},{112,128},... | collective-permute-start | bytes 98312 | tf_op jit(solution)/shard_map/ppermute | solution.py:23
  236.1 80.0 %collective-permute-start.50 = (f32[4,1,1024]{2,1,0:T(1,128)S(1)}, f32[4,1,1024]{2,1,0:T(1,128)S(1)}, u32[]{:S(2)}, u32[]{:S(2)}) collective-permute-start(f32[4,1,1024]{2,1,0:T(1,128)S(1)} %get-tuple-element.140), channel_id=1, source_target_pairs={{1,0},{2,1},{3,2},{4,3},{5,4},{6,5},{7,6},{8,7},{9,8},{10,9},{11,1... | collective-permute-start | bytes 49160 | tf_op jit(solution)/shard_map/ppermute | solution.py:24
  238.0 78.1 %collective-permute-start.51 = (f32[4,1,1024]{2,1,0:T(1,128)S(1)}, f32[4,1,1024]{2,1,0:T(1,128)S(1)}, u32[]{:S(2)}, u32[]{:S(2)}) collective-permute-start(f32[4,1,1024]{2,1,0:T(1,128)S(1)} %get-tuple-element.139), channel_id=1, source_target_pairs={{0,1},{1,2},{2,3},{3,4},{4,5},{5,6},{6,7},{7,8},{8,9},{9,10},{10,1... | collective-permute-start | bytes 49160 | tf_op jit(solution)/shard_map/ppermute | solution.py:23
  381.7 15.8 %collective-permute-start.64 = (f32[1,8,1024]{2,1,0:T(8,128)S(1)}, f32[1,8,1024]{2,1,0:T(8,128)S(1)}, u32[]{:S(2)}, u32[]{:S(2)}) collective-permute-start(f32[1,8,1024]{2,1,0:T(8,128)S(1)} %get-tuple-element.130), channel_id=1, source_target_pairs={{16,0},{32,16},{48,32},{64,48},{80,64},{96,80},{112,96},{128,112},... | collective-permute-start | bytes 98312 | tf_op jit(solution)/shard_map/ppermute | solution.py:24
  398.0 14.8 %collective-permute-start.68 = (f32[1,8,1024]{2,1,0:T(8,128)S(1)}, f32[1,8,1024]{2,1,0:T(8,128)S(1)}, u32[]{:S(2)}, u32[]{:S(2)}) collective-permute-start(f32[1,8,1024]{2,1,0:T(8,128)S(1)} %get-tuple-element.126), channel_id=1, source_target_pairs={{16,0},{32,16},{48,32},{64,48},{80,64},{96,80},{112,96},{128,112},... | collective-permute-start | bytes 98312 | tf_op jit(solution)/shard_map/ppermute | solution.py:24
  414.3 79.9 %collective-permute-start.72 = (f32[1,8,1024]{2,1,0:T(8,128)S(1)}, f32[1,8,1024]{2,1,0:T(8,128)S(1)}, u32[]{:S(2)}, u32[]{:S(2)}) collective-permute-start(f32[1,8,1024]{2,1,0:T(8,128)S(1)} %get-tuple-element.122), channel_id=1, source_target_pairs={{16,0},{32,16},{48,32},{64,48},{80,64},{96,80},{112,96},{128,112},... | collective-permute-start | bytes 98312 | tf_op jit(solution)/shard_map/ppermute | solution.py:24
  415.7 78.5 %collective-permute-start.73 = (f32[1,8,1024]{2,1,0:T(8,128)S(1)}, f32[1,8,1024]{2,1,0:T(8,128)S(1)}, u32[]{:S(2)}, u32[]{:S(2)}) collective-permute-start(f32[1,8,1024]{2,1,0:T(8,128)S(1)} %get-tuple-element.121), channel_id=1, source_target_pairs={{0,16},{16,32},{32,48},{48,64},{64,80},{80,96},{96,112},{112,128},... | collective-permute-start | bytes 98312 | tf_op jit(solution)/shard_map/ppermute | solution.py:23
  419.2 75.0 %collective-permute-start.74 = (f32[4,1,1024]{2,1,0:T(1,128)S(1)}, f32[4,1,1024]{2,1,0:T(1,128)S(1)}, u32[]{:S(2)}, u32[]{:S(2)}) collective-permute-start(f32[4,1,1024]{2,1,0:T(1,128)S(1)} %get-tuple-element.124), channel_id=1, source_target_pairs={{1,0},{2,1},{3,2},{4,3},{5,4},{6,5},{7,6},{8,7},{9,8},{10,9},{11,1... | collective-permute-start | bytes 49160 | tf_op jit(solution)/shard_map/ppermute | solution.py:24
  421.1 73.1 %collective-permute-start.75 = (f32[4,1,1024]{2,1,0:T(1,128)S(1)}, f32[4,1,1024]{2,1,0:T(1,128)S(1)}, u32[]{:S(2)}, u32[]{:S(2)}) collective-permute-start(f32[4,1,1024]{2,1,0:T(1,128)S(1)} %get-tuple-element.123), channel_id=1, source_target_pairs={{0,1},{1,2},{2,3},{3,4},{4,5},{5,6},{6,7},{7,8},{8,9},{9,10},{10,1... | collective-permute-start | bytes 49160 | tf_op jit(solution)/shard_map/ppermute | solution.py:23
  551.2 15.8 %collective-permute-start.88 = (f32[1,8,1024]{2,1,0:T(8,128)S(1)}, f32[1,8,1024]{2,1,0:T(8,128)S(1)}, u32[]{:S(2)}, u32[]{:S(2)}) collective-permute-start(f32[1,8,1024]{2,1,0:T(8,128)S(1)} %get-tuple-element.114), channel_id=1, source_target_pairs={{16,0},{32,16},{48,32},{64,48},{80,64},{96,80},{112,96},{128,112},... | collective-permute-start | bytes 98312 | tf_op jit(solution)/shard_map/ppermute | solution.py:24
  567.5 15.0 %collective-permute-start.92 = (f32[1,8,1024]{2,1,0:T(8,128)S(1)}, f32[1,8,1024]{2,1,0:T(8,128)S(1)}, u32[]{:S(2)}, u32[]{:S(2)}) collective-permute-start(f32[1,8,1024]{2,1,0:T(8,128)S(1)} %get-tuple-element.110), channel_id=1, source_target_pairs={{16,0},{32,16},{48,32},{64,48},{80,64},{96,80},{112,96},{128,112},... | collective-permute-start | bytes 98312 | tf_op jit(solution)/shard_map/ppermute | solution.py:24
  584.1 80.0 %collective-permute-start.96 = (f32[1,8,1024]{2,1,0:T(8,128)S(1)}, f32[1,8,1024]{2,1,0:T(8,128)S(1)}, u32[]{:S(2)}, u32[]{:S(2)}) collective-permute-start(f32[1,8,1024]{2,1,0:T(8,128)S(1)} %get-tuple-element.106), channel_id=1, source_target_pairs={{16,0},{32,16},{48,32},{64,48},{80,64},{96,80},{112,96},{128,112},... | collective-permute-start | bytes 98312 | tf_op jit(solution)/shard_map/ppermute | solution.py:24
  585.4 78.7 %collective-permute-start.97 = (f32[1,8,1024]{2,1,0:T(8,128)S(1)}, f32[1,8,1024]{2,1,0:T(8,128)S(1)}, u32[]{:S(2)}, u32[]{:S(2)}) collective-permute-start(f32[1,8,1024]{2,1,0:T(8,128)S(1)} %get-tuple-element.105), channel_id=1, source_target_pairs={{0,16},{16,32},{32,48},{48,64},{64,80},{80,96},{96,112},{112,128},... | collective-permute-start | bytes 98312 | tf_op jit(solution)/shard_map/ppermute | solution.py:23
  588.8 75.1 %collective-permute-start.98 = (f32[4,1,1024]{2,1,0:T(1,128)S(1)}, f32[4,1,1024]{2,1,0:T(1,128)S(1)}, u32[]{:S(2)}, u32[]{:S(2)}) collective-permute-start(f32[4,1,1024]{2,1,0:T(1,128)S(1)} %get-tuple-element.108), channel_id=1, source_target_pairs={{1,0},{2,1},{3,2},{4,3},{5,4},{6,5},{7,6},{8,7},{9,8},{10,9},{11,1... | collective-permute-start | bytes 49160 | tf_op jit(solution)/shard_map/ppermute | solution.py:24
  590.7 73.3 %collective-permute-start.99 = (f32[4,1,1024]{2,1,0:T(1,128)S(1)}, f32[4,1,1024]{2,1,0:T(1,128)S(1)}, u32[]{:S(2)}, u32[]{:S(2)}) collective-permute-start(f32[4,1,1024]{2,1,0:T(1,128)S(1)} %get-tuple-element.107), channel_id=1, source_target_pairs={{0,1},{1,2},{2,3},{3,4},{4,5},{5,6},{6,7},{7,8},{8,9},{9,10},{10,1... | collective-permute-start | bytes 49160 | tf_op jit(solution)/shard_map/ppermute | solution.py:23
  (134 other events, 3877.6 us)
